TPU v7x, 32 devices: a whole 2x2x4 slice. The times are simulated.
32 devices in a mesh: groups: 2 (over x), tm: 8 (over z, y), site: 2 (over core).
Axes of the slice: x: 2, y: 2, z: 4, core: 2. Of those that a mesh axis runs over, the one named last changes fastest.
Arguments:
- features: float32 [4, 4096, 128], P(('groups', 'site'), 'tm'), parts along dimension 0, may hold values from -18 to 18
- forget: float32 [4, 4096, 128], P(('groups', 'site'), 'tm'), parts along dimension 0, may hold values from 1.2207031e-05 to 0.5, as said below
- labels: int32 [4, 4096], P(('groups', 'site'), 'tm'), parts along dimension 0, may hold values from 0 to 127
- lengths: int32 [4], P(('groups', 'site')), parts along dimension 0, may hold values from 2048 to 4096, as said below
- w_conv: bfloat16 [2, 1024, 1024], P(None, ('tm', 'site')), may hold values from -0.1875 to 0.1875
- w_res: bfloat16 [2, 512, 512], P(None, ('tm', 'site')), may hold values from -0.25 to 0.25
- w_in: bfloat16 [128, 512], P(('tm', 'site')), may hold values from -0.5 to 0.5
- w_out: bfloat16 [512, 128], P(('tm', 'site')), may hold values from -0.25 to 0.25
Outputs:
- row_loss: float32 [4, 4096], P(('groups', 'site'), 'tm'), parts along dimension 0
- grad_conv: float32 [4, 1024, 1024], P('groups', ('tm', 'site')), parts along dimension 0
- grad_res: float32 [4, 512, 512], P('groups', ('tm', 'site')), parts along dimension 0
- grad_in: float32 [128, 1024], P(('tm', 'site'), 'groups'), parts along dimension 1
- grad_out: float32 [512, 256], P(('tm', 'site'), 'groups'), parts along dimension 1
There are 2 independent parts, one for each index of `groups`. A program takes and returns all parts, laid end to end along the dimension named above; an argument that names none is the same for every part. Nothing has to cross between parts.
Inputs may be any that keep to these rules, and one draw needn't show every extreme that they name: `forget`: every entry is positive. `lengths`: at least one site is valid over all 4096 steps.
All inputs are finite; a program needn't handle non-finite values.
Results may differ from a plain program's by a relative error of at most 0.02.
Values may be sent and summed in bfloat16 or wider, within the bound.
A program may use at most 128 MiB of HBM per device.

v0:
```python
import math

import jax
import jax.numpy as jnp
from jax import lax
from jax.sharding import PartitionSpec as P

LAYERS = 2
BASE_DILATION = 256


level_floor = 0.1


def shifted(value, axis, by):
    size = lax.axis_size(axis)
    pairs = [(i, i + by) for i in range(size) if 0 <= i + by < size]
    return lax.ppermute(value, axis, pairs)


def compose(earlier, later):
    retain_first, mass_first, weight_first = earlier
    retain_second, mass_second, weight_second = later
    return (
        retain_first * retain_second,
        retain_second * mass_first + mass_second,
        retain_second * weight_first + weight_second,
    )


def delayed(hidden_now, dilation_step):
    steps_here = hidden_now.shape[1]
    reach_rows = min(dilation_step, steps_here)
    hop_count = -(-dilation_step // steps_here)
    arrived = shifted(hidden_now[:, steps_here - reach_rows :], "tm", hop_count)
    return jnp.concatenate([arrived, hidden_now[:, : steps_here - reach_rows]], axis=1)


def advanced(past_grad, dilation_step):
    steps_here = past_grad.shape[1]
    reach_rows = min(dilation_step, steps_here)
    hop_count = -(-dilation_step // steps_here)
    arrived = shifted(past_grad[:, :reach_rows].astype(jnp.bfloat16), "tm", -hop_count).astype(
        jnp.float32
    )
    return jnp.concatenate([past_grad[:, reach_rows:], arrived], axis=1)


def on_device(features, forget, labels, lengths, w_conv, w_res, w_in, w_out):
    site_count, steps_here, band_count = features.shape
    row_count = site_count * steps_here
    time_devices = lax.axis_size("tm")
    site_devices = lax.axis_size("site")
    retain = 1.0 - forget
    inflow = forget * (features * features)
    within = lax.associative_scan(compose, (retain, inflow, forget), axis=1)
    summary = (within[0][:, -1], within[1][:, -1], within[2][:, -1])
    identity = (jnp.ones_like(summary[0]), jnp.zeros_like(summary[1]), jnp.zeros_like(summary[2]))
    gathered = (
        lax.all_gather(summary[0], "tm", axis=0, tiled=True),
        lax.all_gather(summary[1], "tm", axis=0, tiled=True),
        lax.all_gather(summary[2], "tm", axis=0, tiled=True),
    )
    shaped = tuple((member.reshape(time_devices, site_count, band_count) for member in gathered))
    inclusive = lax.associative_scan(compose, shaped, axis=0)
    position = lax.axis_index("tm")
    before = jnp.maximum(position - 1, 0)
    carried = tuple(
        (
            jnp.where(
                position > 0, lax.dynamic_index_in_dim(member, before, 0, keepdims=False), neutral
            )
            for member, neutral in zip(inclusive, identity)
        )
    )
    mass_sum = within[0] * carried[1][:, None, :] + within[1]
    weight_sum = within[0] * carried[2][:, None, :] + within[2]
    smoothed = mass_sum / weight_sum
    normed = (features / jnp.sqrt(smoothed + level_floor)).astype(jnp.bfloat16)
    flat_normed = normed.reshape(row_count, band_count)
    conv_all, res_all, in_all, out_all = (
        lax.all_gather(w_conv, ("tm", "site"), axis=1, tiled=True),
        lax.all_gather(w_res, ("tm", "site"), axis=1, tiled=True),
        lax.all_gather(w_in, ("tm", "site"), axis=0, tiled=True),
        lax.all_gather(w_out, ("tm", "site"), axis=0, tiled=True),
    )
    channels = res_all.shape[1]
    hidden_now = jnp.dot(flat_normed, in_all, preferred_element_type=jnp.float32).astype(
        jnp.bfloat16
    )
    hidden_now = hidden_now.reshape(site_count, steps_here, channels)
    saved_layers = []
    for index_of_layer in range(LAYERS):
        dilation_step = BASE_DILATION * 2**index_of_layer
        joined = jnp.concatenate([delayed(hidden_now, dilation_step), hidden_now], axis=2).reshape(
            row_count, 2 * channels
        )
        preact = jnp.dot(joined, conv_all[index_of_layer], preferred_element_type=jnp.float32)
        tanh_part = jnp.tanh(preact[:, :channels])
        sigm_part = jax.nn.sigmoid(preact[:, channels:])
        gated_out = (tanh_part * sigm_part).astype(jnp.bfloat16)
        updated = hidden_now.reshape(row_count, channels).astype(jnp.float32) + jnp.dot(
            gated_out, res_all[index_of_layer], preferred_element_type=jnp.float32
        )
        saved_layers.append((joined, tanh_part, sigm_part, gated_out))
        hidden_now = updated.astype(jnp.bfloat16).reshape(site_count, steps_here, channels)
    flat_hidden = hidden_now.reshape(row_count, channels)
    logits = jnp.dot(flat_hidden, out_all, preferred_element_type=jnp.float32)
    classes = logits.shape[1]
    log_total = jnp.log(jnp.sum(jnp.exp(logits), axis=1))
    target_hot = (labels.reshape(row_count)[:, None] == jnp.arange(classes)[None, :]).astype(
        jnp.float32
    )
    picked = jnp.sum(logits * target_hot, axis=1)
    positions = lax.axis_index("tm") * steps_here + jnp.arange(steps_here)
    validity = (positions[None, :] < lengths[:, None]).astype(jnp.float32)
    row_loss = (log_total - picked).reshape(site_count, steps_here) * validity
    loss_scale = 1.0 / math.sqrt(site_count * site_devices * steps_here * time_devices)
    class_probs = jnp.exp(logits - log_total[:, None])
    logit_grad = (
        (class_probs - target_hot) * (validity.reshape(row_count, 1) * loss_scale)
    ).astype(jnp.bfloat16)
    term_out = jnp.dot(flat_hidden.T, logit_grad, preferred_element_type=jnp.float32)
    gradient = jnp.dot(logit_grad, out_all.T, preferred_element_type=jnp.float32)
    conv_terms = []
    res_terms = []
    for index_of_layer in reversed(range(LAYERS)):
        dilation_step = BASE_DILATION * 2**index_of_layer
        joined, tanh_part, sigm_part, gated_out = saved_layers[index_of_layer]
        rounded = gradient.astype(jnp.bfloat16)
        res_terms.append(jnp.dot(gated_out.T, rounded, preferred_element_type=jnp.float32))
        gated_grad = jnp.dot(rounded, res_all[index_of_layer].T, preferred_element_type=jnp.float32)
        filter_grad = gated_grad * sigm_part * (1.0 - tanh_part * tanh_part)
        gate_grad = gated_grad * tanh_part * sigm_part * (1.0 - sigm_part)
        preact_grad = jnp.concatenate([filter_grad, gate_grad], axis=1).astype(jnp.bfloat16)
        conv_terms.append(jnp.dot(joined.T, preact_grad, preferred_element_type=jnp.float32))
        joined_grad = jnp.dot(
            preact_grad, conv_all[index_of_layer].T, preferred_element_type=jnp.float32
        )
        past_grad = joined_grad[:, :channels].reshape(site_count, steps_here, channels)
        gradient = (
            gradient
            + joined_grad[:, channels:]
            + advanced(past_grad, dilation_step).reshape(row_count, channels)
        )
    term_in = jnp.dot(
        flat_normed.T, gradient.astype(jnp.bfloat16), preferred_element_type=jnp.float32
    )
    term_conv = jnp.stack(conv_terms[::-1])
    term_res = jnp.stack(res_terms[::-1])
    grad_conv, grad_res, grad_in, grad_out = (
        lax.psum_scatter(term_conv, ("tm", "site"), scatter_dimension=1, tiled=True),
        lax.psum_scatter(term_res, ("tm", "site"), scatter_dimension=1, tiled=True),
        lax.psum_scatter(term_in, ("tm", "site"), scatter_dimension=0, tiled=True),
        lax.psum_scatter(term_out, ("tm", "site"), scatter_dimension=0, tiled=True),
    )
    return (row_loss, grad_conv, grad_res, grad_in, grad_out)


def solution(mesh):
    return jax.shard_map(
        on_device,
        mesh=mesh,
        in_specs=(
            P(("groups", "site"), "tm", None),
            P(("groups", "site"), "tm", None),
            P(("groups", "site"), "tm"),
            P(("groups", "site")),
            P(None, ("tm", "site"), None),
            P(None, ("tm", "site"), None),
            P(("tm", "site"), None),
            P(("tm", "site"), None),
        ),
        out_specs=(
            P(("groups", "site"), "tm"),
            P("groups", ("tm", "site"), None),
            P("groups", ("tm", "site"), None),
            P(("tm", "site"), "groups"),
            P(("tm", "site"), "groups"),
        ),
        check_vma=False,
    )
```

profile of v0, /device:TPU:0, one launch (start us, length us, event | category | flops | bytes accessed | tf_op | source)
XLA Modules:
  0.0 466.4 jit_solution(17393127125160778999)
XLA Ops:
  7.2 0.7 all-gather.6.cloned.1.call-update
  7.9 0.7 all-gather.8.cloned.1.call-update
  8.7 0.7 slice.668
  9.4 1.0 slice.669
  10.4 1.0 slice.709
  11.3 1.0 slice.670
  12.3 1.1 multiply_multiply_fusion
  17.6 22.3 %all-gather.1 = f32[8,1,128]{2,1,0:T(1,128)S(1)} all-gather(f32[1,1,128]{2,1,0:T(1,128)S(1)} %slice_add_fusion.11), channel_id=3, replica_groups=mesh['groups'=2,'tm'=8,'site'=2] {'tm'}, dimensions={0}, use_global_device_ids=true | all-gather | bytes 4608 | tf_op jit(solution)/shard_map/all_gather | solution.py:60
  40.0 16.7 %all-gather.2 = f32[8,1,128]{2,1,0:T(1,128)S(1)} all-gather(f32[1,1,128]{2,1,0:T(1,128)S(1)} %slice_add_fusion.8), channel_id=4, replica_groups=mesh['groups'=2,'tm'=8,'site'=2] {'tm'}, dimensions={0}, use_global_device_ids=true | all-gather | bytes 4608 | tf_op jit(solution)/shard_map/all_gather | solution.py:62
  56.7 18.2 %all-gather = f32[8,1,128]{2,1,0:T(1,128)S(1)} all-gather(f32[1,1,128]{2,1,0:T(1,128)S(1)} %slice_add_fusion.12), channel_id=2, replica_groups=mesh['groups'=2,'tm'=8,'site'=2] {'tm'}, dimensions={0}, use_global_device_ids=true | all-gather | bytes 4608 | tf_op jit(solution)/shard_map/all_gather | solution.py:61
  75.5 17.6 %all_gather.24 = bf16[128,512]{1,0:T(8,128)(2,1)S(1)} all-gather(bf16[8,512]{1,0:T(8,128)(2,1)S(1)} %copy-done.13), channel_id=1, replica_groups=mesh['groups'=2,'tm'=8,'site'=2] {'tm','site'}, dimensions={0}, use_global_device_ids=true | all-gather | bytes 139264 | tf_op jit(solution)/shard_map/all_gather | solution.py:84
  93.6 3.9 collective-permute-start
  97.5 6.0 %collective-permute-done = bf16[1,256,512]{1,2,0:T(8,128)(2,1)S(1)} collective-permute-done((bf16[1,256,512]{1,2,0:T(8,128)(2,1)S(1)}, bf16[1,256,512]{1,2,0:T(8,128)(2,1)S(1)}, u32[]{:S(2)}, u32[]{:S(2)}) %collective-permute-start) | collective-permute-done | bytes 262176 | tf_op jit(solution)/shard_map/ppermute | solution.py:18
  103.6 0.7 copy-done.21
  104.3 2.9 fusion.1
  107.2 1.4 copy-done.4
  109.0 1.7 fusion.4
  110.7 4.4 collective-permute-start.1
  115.8 23.5 %all_gather.27 = bf16[512,128]{1,0:T(8,128)(2,1)S(1)} all-gather(bf16[32,128]{1,0:T(8,128)(2,1)S(1)} %copy-done.14), channel_id=1, replica_groups=mesh['groups'=2,'tm'=8,'site'=2] {'tm','site'}, dimensions={0}, use_global_device_ids=true | all-gather | bytes 139264 | tf_op jit(solution)/shard_map/all_gather | solution.py:85
  139.3 3.1 fusion.3
  142.9 0.8 copy-done.16
  143.6 0.5 fusion.5
  144.8 0.8 multiply_convert_fusion.3
  145.7 1.7 copy-done.15
  147.4 1.3 fusion.2
  148.8 1.6 collective-permute-start.2
  150.4 14.6 %collective-permute-done.2 = bf16[1,512,512]{2,1,0:T(8,128)(2,1)S(1)} collective-permute-done((bf16[1,512,512]{2,1,0:T(8,128)(2,1)S(1)}, bf16[1,512,512]{2,1,0:T(8,128)(2,1)S(1)}, u32[]{:S(2)}, u32[]{:S(2)}) %collective-permute-start.2) | collective-permute-done | bytes 524320 | tf_op jit(solution)/shard_map/ppermute | solution.py:18
  165.3 0.8 multiply_convert_fusion.1
  166.1 1.3 fusion
  167.4 1.3 copy-done.6
  168.9 0.7 slice.1024
  169.6 1.3 collective-permute-start.3
  170.9 1.0 fusion.54
  172.1 7.3 %collective-permute-done.3 = bf16[1,256,512]{2,1,0:T(8,128)(2,1)S(1)} collective-permute-done((bf16[1,256,512]{2,1,0:T(8,128)(2,1)}, bf16[1,256,512]{2,1,0:T(8,128)(2,1)S(1)}, u32[]{:S(2)}, u32[]{:S(2)}) %collective-permute-start.3) | collective-permute-done | bytes 262176 | tf_op jit(solution)/shard_map/ppermute | solution.py:18
  179.5 2.4 fusion.16
  182.0 0.5 convolution_bitcast_fusion.2
  182.4 0.5 copy-done.1
  182.9 0.5 convolution_bitcast_fusion.3
  183.4 1.5 pad_maximum_fusion.1
  185.0 0.9 copy-done.18
  186.4 1.2 convolution_bitcast_fusion
  187.7 1.2 convolution_bitcast_fusion.1
  189.0 4.2 pad_maximum_fusion
  193.2 0.6 compare_select_fusion
  193.8 35.1 %reduce-scatter.11.cloned.1.call-done = f32[32,128]{1,0:T(8,128)} async-done(((f32[512,128]{1,0:T(8,128)}), f32[32,128]{1,0:T(8,128)}) %reduce-scatter.11.cloned.1.call-update) | async-done | bytes 16400 | tf_op jit(solution)/shard_map/reduce_scatter | solution.py:155
  228.9 58.8 %reduce-scatter.9.cloned.1.call-done = f32[8,512]{1,0:T(8,128)} async-done(((f32[128,512]{1,0:T(8,128)}), f32[8,512]{1,0:T(8,128)}) %reduce-scatter.9.cloned.1.call-update) | async-done | bytes 16400 | tf_op jit(solution)/shard_map/reduce_scatter | solution.py:154
  287.7 65.1 %reduce-scatter.7.cloned.1.call-done = f32[2,32,512]{2,1,0:T(8,128)} async-done(((f32[2,512,512]{2,1,0:T(8,128)}), f32[2,32,512]{2,1,0:T(8,128)}) %reduce-scatter.7.cloned.1.call-update) | async-done | bytes 131088 | tf_op jit(solution)/shard_map/reduce_scatter | solution.py:153
  352.7 106.9 %reduce-scatter.5.cloned.1.call-done = f32[2,64,1024]{2,1,0:T(8,128)} async-done(((f32[2,1024,1024]{2,1,0:T(8,128)}), f32[2,64,1024]{2,1,0:T(8,128)}) %reduce-scatter.5.cloned.1.call-update) | async-done | bytes 524304 | tf_op jit(solution)/shard_map/reduce_scatter | solution.py:152
  (308 shorter events, 7.1 us)
Async XLA Ops:
  7.2 96.4 %all-gather.6.cloned.1.call-start = ((), (), s32[]{:S(2)}) async-start(), calls=%async_computation.4 | async-start | bytes 4456448 | tf_op jit(solution)/shard_map/all_gather | solution.py:82
  7.9 101.1 %all-gather.8.cloned.1.call-start = ((), (), s32[]{:S(2)}) async-start(), calls=%async_computation.5 | async-start | bytes 1114112 | tf_op jit(solution)/shard_map/all_gather | solution.py:83
  8.6 220.2 %reduce-scatter.11.cloned.1.call-start = ((), (), s32[]{:S(2)}) async-start(), calls=%async_computation.9 | async-start | bytes 278528 | tf_op jit(solution)/shard_map/reduce_scatter | solution.py:155
  17.3 58.2 %copy-start.13 = (bf16[8,512]{1,0:T(8,128)(2,1)S(1)}, bf16[8,512]{1,0:T(8,128)(2,1)}, u32[]{:S(2)}) copy-start(bf16[8,512]{1,0:T(8,128)(2,1)} %param.14) | copy-start | bytes 24580
  17.4 75.7 %copy-start.9 = (f32[1,512,128]{2,1,0:T(8,128)S(1)}, f32[1,512,128]{2,1,0:T(8,128)}, u32[]{:S(2)}) copy-start(f32[1,512,128]{2,1,0:T(8,128)} %param.8) | copy-start | bytes 786436
  93.6 15.4 %copy-start.7 = (bf16[512,512]{0,1:T(8,128)(2,1)}, bf16[512,512]{0,1:T(8,128)(2,1)S(1)}, u32[]{:S(2)}) copy-start(bf16[512,512]{0,1:T(8,128)(2,1)S(1)} %convolution_convert_fusion) | copy-start | bytes 1572868
  93.6 9.9 %copy-start.10 = (bf16[1,256,512]{1,2,0:T(8,128)(2,1)}, bf16[1,256,512]{1,2,0:T(8,128)(2,1)S(1)}, u32[]{:S(2)}) copy-start(bf16[1,256,512]{1,2,0:T(8,128)(2,1)S(1)} %get-tuple-element.12) | copy-start | bytes 786436
  93.6 9.9 %collective-permute-start = (bf16[1,256,512]{1,2,0:T(8,128)(2,1)S(1)}, bf16[1,256,512]{1,2,0:T(8,128)(2,1)S(1)}, u32[]{:S(2)}, u32[]{:S(2)}) collective-permute-start(bf16[1,256,512]{1,2,0:T(8,128)(2,1)S(1)} %get-tuple-element.11), channel_id=1, source_target_pairs={{0,2},{2,4},{4,6},{6,8},{8,10},{10,12},{12,14},{1,3},{3,5},{5,7},{... | collective-permute-start | bytes 786440 | tf_op jit(solution)/shard_map/ppermute | solution.py:18
  103.6 0.7 copy-start.21
  107.2 1.4 copy-start.4
  108.5 7.3 %copy-start.14 = (bf16[32,128]{1,0:T(8,128)(2,1)S(1)}, bf16[32,128]{1,0:T(8,128)(2,1)}, u32[]{:S(2)}) copy-start(bf16[32,128]{1,0:T(8,128)(2,1)} %param.15) | copy-start | bytes 24580
  109.0 33.4 %copy-start = (bf16[512,512]{1,0:T(8,128)(2,1)}, bf16[512,512]{1,0:T(8,128)(2,1)S(1)}, u32[]{:S(2)}) copy-start(bf16[512,512]{1,0:T(8,128)(2,1)S(1)} %multiply_convert_fusion.5) | copy-start | bytes 1572868
  110.7 32.2 %copy-start.17 = (bf16[512,512]{0,1:T(8,128)(2,1)}, bf16[512,512]{0,1:T(8,128)(2,1)S(1)}, u32[]{:S(2)}) copy-start(bf16[512,512]{0,1:T(8,128)(2,1)S(1)} %fusion.4) | copy-start | bytes 1572868
  110.7 28.6 %collective-permute-start.1 = (bf16[1,512,512]{1,2,0:T(8,128)(2,1)S(1)}, bf16[1,512,512]{1,2,0:T(8,128)(2,1)S(1)}, u32[]{:S(2)}, u32[]{:S(2)}) collective-permute-start(bf16[1,512,512]{1,2,0:T(8,128)(2,1)S(1)} %bitcast.80), channel_id=1, source_target_pairs={{0,2},{2,4},{4,6},{6,8},{8,10},{10,12},{12,14},{1,3},{3,5},{5,7},{... | collective-permute-start | bytes 1572872 | tf_op jit(solution)/shard_map/ppermute | solution.py:18
  139.3 3.1 copy-start.19
  142.4 1.2 copy-start.16
  142.4 1.7 copy-start.12
  143.6 0.8 copy-start.2
  144.8 2.6 copy-start.15
  145.7 3.0 copy-start.23
  145.7 3.0 copy-start.25
  148.8 16.5 %copy-start.5 = (f32[512,1024]{1,0:T(8,128)S(1)}, f32[512,1024]{1,0:T(8,128)}, u32[]{:S(2)}) copy-start(f32[512,1024]{1,0:T(8,128)} %copy-done.4) | copy-start | bytes 6291460
  148.8 16.2 %collective-permute-start.2 = (bf16[1,512,512]{2,1,0:T(8,128)(2,1)S(1)}, bf16[1,512,512]{2,1,0:T(8,128)(2,1)S(1)}, u32[]{:S(2)}, u32[]{:S(2)}) collective-permute-start(bf16[1,512,512]{2,1,0:T(8,128)(2,1)S(1)} %fusion.15), channel_id=1, source_target_pairs={{2,0},{4,2},{6,4},{8,6},{10,8},{12,10},{14,12},{3,1},{5,3},{7,5},{... | collective-permute-start | bytes 1572872 | tf_op jit(solution)/shard_map/ppermute | solution.py:18
  166.1 1.3 copy-start.27
  166.1 1.3 copy-start.29
  167.4 1.3 copy-start.6
  169.6 9.8 %collective-permute-start.3 = (bf16[1,256,512]{2,1,0:T(8,128)(2,1)}, bf16[1,256,512]{2,1,0:T(8,128)(2,1)S(1)}, u32[]{:S(2)}, u32[]{:S(2)}) collective-permute-start(bf16[1,256,512]{2,1,0:T(8,128)(2,1)} %slice.1024), channel_id=1, source_target_pairs={{2,0},{4,2},{6,4},{8,6},{10,8},{12,10},{14,12},{3,1},{5,3},{7,5},{... | collective-permute-start | bytes 786440 | tf_op jit(solution)/shard_map/ppermute | solution.py:18
  172.0 115.7 %reduce-scatter.9.cloned.1.call-start = ((), (), s32[]{:S(2)}) async-start(), calls=%async_computation.8 | async-start | bytes 278528 | tf_op jit(solution)/shard_map/reduce_scatter | solution.py:154
  179.5 2.5 copy-start.3
  181.9 1.0 copy-start.1
  181.9 170.8 %reduce-scatter.7.cloned.1.call-start = ((), (), s32[]{:S(2)}) async-start(), calls=%async_computation.7 | async-start | bytes 2228224 | tf_op jit(solution)/shard_map/reduce_scatter | solution.py:153
  184.9 1.0 copy-start.18
  184.9 1.2 copy-start.20
  184.9 1.4 copy-start.24
  184.9 1.5 copy-start.26
  184.9 2.8 copy-start.8
  184.9 2.8 copy-start.11
  185.0 2.8 copy-start.22
  185.0 274.6 %reduce-scatter.5.cloned.1.call-start = ((), (), s32[]{:S(2)}) async-start(), calls=%async_computation.6 | async-start | bytes 8912896 | tf_op jit(solution)/shard_map/reduce_scatter | solution.py:152
  186.4 1.3 copy-start.28
  186.4 1.3 copy-start.30
Sparse Core Ops, SparseCore 0:
  10.2 53.1 all-gather.5
  65.6 36.4 all-gather.7
  172.1 56.7 reduce-scatter.10
  232.8 54.7 reduce-scatter.8
  291.8 60.8 reduce-scatter.6
  357.2 102.3 reduce-scatter.4
where the time goes:
time: 467 us; the launch traced here: 466 us
  waiting for transfers between devices  295 us (63%)
  blocking collectives  98.3 us (21%)
  matrix products  20.2 us (4%)
  between operations  16.4 us (4%)
  local copies, waits for them, and re-layouts  15.2 us (3%)
  starting transfers between devices  11.4 us (2%)
  other arithmetic  9.54 us (2%)
    reduce_scatter x1, waiting for transfers between devices, on_device(): lax.psum_scatter(term_conv, ('tm', 'site'), scatter_dimension=1, tiled=True)  107 us
    reduce_scatter x1, waiting for transfers between devices, on_device(): lax.psum_scatter(term_res, ('tm', 'site'), scatter_dimension=1, tiled=True)  65.1 us
    reduce_scatter x1, waiting for transfers between devices, on_device(): lax.psum_scatter(term_in, ('tm', 'site'), scatter_dimension=0, tiled=True)  58.8 us
    reduce_scatter x1, waiting for transfers between devices, on_device(): lax.psum_scatter(term_out, ('tm', 'site'), scatter_dimension=0, tiled=True)  35.1 us
    ppermute x4, waiting for transfers between devices, shifted(): return lax.ppermute(value, axis, pairs)  28 us
    all_gather x1, blocking collectives, on_device(): lax.all_gather(w_out, ('tm', 'site'), axis=0, tiled=True)  23.5 us
    all_gather x1, blocking collectives, on_device(): lax.all_gather(summary[0], 'tm', axis=0, tiled=True)  22.3 us
    all_gather x1, blocking collectives, on_device(): lax.all_gather(summary[1], 'tm', axis=0, tiled=True)  18.2 us
  transfers between devices with their start and end apart: 10, of which 7 were waited for; matrix products, arithmetic and copies ran while one was open for 5% of the time, Pallas kernels for 0%

commit v1 on v0

--- a/solution.py
+++ b/solution.py
@@ -44,6 +44,55 @@
         jnp.float32
     )
     return jnp.concatenate([past_grad[:, reach_rows:], arrived], axis=1)
+
+
+def gather_weights(*weights):
+    shard_devices = lax.axis_size("tm") * lax.axis_size("site")
+    flat = jnp.concatenate([w.reshape(-1) for w in weights])
+    stacked = lax.all_gather(flat, ("tm", "site"), axis=0, tiled=False)
+    full = []
+    start = 0
+    for w in weights:
+        size = w.size
+        piece = stacked[:, start : start + size]
+        start += size
+        if w.ndim == 3:
+            piece = piece.reshape(shard_devices, w.shape[0], w.shape[1], w.shape[2])
+            piece = piece.transpose(1, 0, 2, 3).reshape(
+                w.shape[0], shard_devices * w.shape[1], w.shape[2]
+            )
+        else:
+            piece = piece.reshape(shard_devices * w.shape[0], w.shape[1])
+        full.append(piece)
+    return full
+
+
+def scatter_terms(*terms):
+    shard_devices = lax.axis_size("tm") * lax.axis_size("site")
+    flat = []
+    for t in terms:
+        if t.ndim == 3:
+            piece = t.reshape(t.shape[0], shard_devices, t.shape[1] // shard_devices, t.shape[2])
+            piece = piece.transpose(1, 0, 2, 3)
+        else:
+            piece = t
+        flat.append(piece.reshape(shard_devices, -1).astype(jnp.bfloat16))
+    joined_terms = jnp.concatenate(flat, axis=1)
+    reduced = lax.psum_scatter(
+        joined_terms.reshape(shard_devices * 64, -1), ("tm", "site"), scatter_dimension=0, tiled=True
+    ).astype(jnp.float32).reshape(-1)
+    out = []
+    start = 0
+    for t in terms:
+        size = t.size // shard_devices
+        piece = reduced[start : start + size]
+        start += size
+        if t.ndim == 3:
+            piece = piece.reshape(t.shape[0], t.shape[1] // shard_devices, t.shape[2])
+        else:
+            piece = piece.reshape(t.shape[0] // shard_devices, t.shape[1])
+        out.append(piece)
+    return out
 
 
 def on_device(features, forget, labels, lengths, w_conv, w_res, w_in, w_out):
@@ -56,12 +105,8 @@
     within = lax.associative_scan(compose, (retain, inflow, forget), axis=1)
     summary = (within[0][:, -1], within[1][:, -1], within[2][:, -1])
     identity = (jnp.ones_like(summary[0]), jnp.zeros_like(summary[1]), jnp.zeros_like(summary[2]))
-    gathered = (
-        lax.all_gather(summary[0], "tm", axis=0, tiled=True),
-        lax.all_gather(summary[1], "tm", axis=0, tiled=True),
-        lax.all_gather(summary[2], "tm", axis=0, tiled=True),
-    )
-    shaped = tuple((member.reshape(time_devices, site_count, band_count) for member in gathered))
+    packed = lax.all_gather(jnp.stack(summary), "tm", axis=0, tiled=False)
+    shaped = tuple(packed[:, index] for index in range(3))
     inclusive = lax.associative_scan(compose, shaped, axis=0)
     position = lax.axis_index("tm")
     before = jnp.maximum(position - 1, 0)
@@ -78,12 +123,7 @@
     smoothed = mass_sum / weight_sum
     normed = (features / jnp.sqrt(smoothed + level_floor)).astype(jnp.bfloat16)
     flat_normed = normed.reshape(row_count, band_count)
-    conv_all, res_all, in_all, out_all = (
-        lax.all_gather(w_conv, ("tm", "site"), axis=1, tiled=True),
-        lax.all_gather(w_res, ("tm", "site"), axis=1, tiled=True),
-        lax.all_gather(w_in, ("tm", "site"), axis=0, tiled=True),
-        lax.all_gather(w_out, ("tm", "site"), axis=0, tiled=True),
-    )
+    conv_all, res_all, in_all, out_all = gather_weights(w_conv, w_res, w_in, w_out)
     channels = res_all.shape[1]
     hidden_now = jnp.dot(flat_normed, in_all, preferred_element_type=jnp.float32).astype(
         jnp.bfloat16
@@ -148,12 +188,7 @@
     )
     term_conv = jnp.stack(conv_terms[::-1])
     term_res = jnp.stack(res_terms[::-1])
-    grad_conv, grad_res, grad_in, grad_out = (
-        lax.psum_scatter(term_conv, ("tm", "site"), scatter_dimension=1, tiled=True),
-        lax.psum_scatter(term_res, ("tm", "site"), scatter_dimension=1, tiled=True),
-        lax.psum_scatter(term_in, ("tm", "site"), scatter_dimension=0, tiled=True),
-        lax.psum_scatter(term_out, ("tm", "site"), scatter_dimension=0, tiled=True),
-    )
+    grad_conv, grad_res, grad_in, grad_out = scatter_terms(term_conv, term_res, term_in, term_out)
     return (row_loss, grad_conv, grad_res, grad_in, grad_out)
 
 

time: 467 us -> 270 us (0.58)
  waiting for transfers between devices: 295 us -> 125 us
  blocking collectives: 98.3 us -> 28.2 us
  local copies, waits for them, and re-layouts: 15.2 us -> 47.3 us
  other arithmetic: 9.54 us -> 26.1 us
    reduce_scatter x4 -> x1, waiting for transfers between devices: 266 us -> 79.9 us  [scatter_terms(): lax.psum_scatter(joined_terms.reshape(shard_devices * 64, -1), ('tm', 'si...]
    all_gather x5 -> x1, blocking collectives: 98.3 us -> 28.2 us  [on_device(): packed = lax.all_gather(jnp.stack(summary), 'tm', axis=0, tiled=False)]
    all_gather x2 -> x1, waiting for transfers between devices: 0.02 us -> 24.1 us  [gather_weights(): stacked = lax.all_gather(flat, ('tm', 'site'), axis=0, tiled=False)]
    concatenate x0 -> x4, other arithmetic: none -> 22.8 us  [the longest x1 18.1 us: scatter_terms(): joined_terms = jnp.concatenate(flat, axis=1)]
    slice x0 -> x12, local copies, waits for them, and re-layouts: none -> 9.41 us  [the longest x4 5.47 us: gather_weights(): piece = stacked[:, start:start + size]]
    reshape x0 -> x6, local copies, waits for them, and re-layouts: none -> 8.91 us  [the longest x1 5.78 us: scatter_terms(): joined_terms.reshape(shard_devices * 64, -1)]
    unnamed x62 -> x37, local copies, waits for them, and re-layouts: 7.86 us -> 16.7 us
    ppermute x4, waiting for transfers between devices: 28 us -> 20.7 us  [shifted(): return lax.ppermute(value, axis, pairs)]
  transfers between devices with their start and end apart: 10 -> 6, of which waited for: 7 -> 5; matrix products, arithmetic and copies ran while one was open for 5% -> 9% of each run, Pallas kernels for 0% -> 0%
where the time goes in v1:
time: 270 us; the launch traced here: 269 us
  waiting for transfers between devices  125 us (46%)
  local copies, waits for them, and re-layouts  47.3 us (18%)
  blocking collectives  28.2 us (10%)
  other arithmetic  26.1 us (10%)
  between operations  16.4 us (6%)
  matrix products  15.7 us (6%)
  starting transfers between devices  10.5 us (4%)
    reduce_scatter x1, waiting for transfers between devices, scatter_terms(): lax.psum_scatter(joined_terms.reshape(shard_devices * 64, -1), ('tm', 'si...  79.9 us
    all_gather x1, blocking collectives, on_device(): packed = lax.all_gather(jnp.stack(summary), 'tm', axis=0, tiled=False)  28.2 us
    all_gather x1, waiting for transfers between devices, gather_weights(): stacked = lax.all_gather(flat, ('tm', 'site'), axis=0, tiled=False)  24.1 us
    ppermute x4, waiting for transfers between devices, shifted(): return lax.ppermute(value, axis, pairs)  20.7 us
    concatenate x1, other arithmetic, scatter_terms(): joined_terms = jnp.concatenate(flat, axis=1)  18.1 us
    unnamed x37, local copies, waits for them, and re-layouts  16.7 us
    ppermute x4, starting transfers between devices, shifted(): return lax.ppermute(value, axis, pairs)  10.4 us
    reshape x1, local copies, waits for them, and re-layouts, scatter_terms(): joined_terms.reshape(shard_devices * 64, -1)  5.78 us
  transfers between devices with their start and end apart: 6, of which 5 were waited for; matrix products, arithmetic and copies ran while one was open for 9% of the time, Pallas kernels for 0%

profile of v1, /device:TPU:0, one launch (start us, length us, event | category | flops | bytes accessed | tf_op | source)
XLA Modules:
  0.0 269.0 jit_solution(2828392130204439528)
XLA Ops:
  7.2 0.7 copy.87
  8.0 0.9 copy.86
  8.8 1.0 copy.85
  9.9 1.5 pad_maximum_fusion.10
  11.4 0.7 slice.693
  12.1 1.0 slice.694
  13.0 1.0 slice.734
  18.5 28.2 %all-gather = f32[24,1,128]{2,1,0:T(1,128)S(1)} all-gather(f32[3,1,128]{2,1,0:T(1,128)S(1)} %pad_maximum_fusion.34), channel_id=2, replica_groups=mesh['groups'=2,'tm'=8,'site'=2] {'tm'}, dimensions={0}, use_global_device_ids=true | all-gather | bytes 13824 | tf_op jit(solution)/shard_map/all_gather | solution.py:108
  47.3 24.1 %all-gather.4.cloned.1.call-done = bf16[2752512]{0:T(1024)(128)(2,1)} async-done(((bf16[172032]{0:T(1024)(128)(2,1)}), bf16[2752512]{0:T(1024)(128)(2,1)}) %all-gather.4.cloned.1.call-update) | async-done | bytes 5505040 | tf_op jit(solution)/shard_map/all_gather | solution.py:52
  71.4 5.6 %reshape.213 = bf16[16,172032]{1,0:T(8,128)(2,1)} reshape(bf16[2752512]{0:T(1024)(128)(2,1)} %all-gather.4.cloned.1.call-done) | data formatting | bytes 11010048 | tf_op jit(solution)/shard_map/all_gather | solution.py:52
  77.0 1.0 fusion.56
  78.0 4.5 %slice.878 = bf16[16,131072]{1,0:T(8,128)(2,1)} slice(bf16[16,172032]{1,0:T(8,128)(2,1)} %reshape.213), slice={[0:16], [0:131072]} | slice | bytes 8388608 | tf_op jit(solution)/shard_map/slice | solution.py:57
  83.0 2.5 collective-permute-start
  85.5 4.6 %copy.88 = bf16[2,8,128,1024]{3,2,1,0:T(8,128)(2,1)S(1)} copy(bf16[2,8,128,1024]{3,1,2,0:T(8,128)(2,1)} %bitcast.126) | data formatting | bytes 8388608
  90.4 1.8 fusion.57
  92.3 0.8 copy-done.13
  93.2 1.3 fusion.15
  94.9 0.5 fusion
  95.8 5.1 %collective-permute-start.1 = (bf16[1,512,512]{1,2,0:T(8,128)(2,1)S(1)}, bf16[1,512,512]{1,2,0:T(8,128)(2,1)}, u32[]{:S(2)}, u32[]{:S(2)}) collective-permute-start(bf16[1,512,512]{1,2,0:T(8,128)(2,1)S(1)} %bitcast.132), channel_id=1, source_target_pairs={{0,2},{2,4},{4,6},{6,8},{8,10},{10,12},{12,14},{1,3},{3,5},{5,7},{... | collective-permute-start | bytes 1572872 | tf_op jit(solution)/shard_map/ppermute | solution.py:18
  101.7 2.1 pad_maximum_fusion.1
  103.8 7.6 %collective-permute-done.1 = bf16[1,512,512]{1,2,0:T(8,128)(2,1)} collective-permute-done((bf16[1,512,512]{1,2,0:T(8,128)(2,1)S(1)}, bf16[1,512,512]{1,2,0:T(8,128)(2,1)}, u32[]{:S(2)}, u32[]{:S(2)}) %collective-permute-start.1) | collective-permute-done | bytes 524320 | tf_op jit(solution)/shard_map/ppermute | solution.py:18
  111.4 2.3 fusion.13
  114.2 0.5 fusion.1
  116.2 2.7 multiply_convert_fusion.3
  118.9 1.3 fusion.18
  120.3 1.3 collective-permute-start.2
  121.6 1.1 pad_maximum_fusion.2
  123.2 1.2 convert_bitcast_fusion
  124.4 11.5 %collective-permute-done.2 = bf16[1,512,512]{2,1,0:T(8,128)(2,1)S(1)} collective-permute-done((bf16[1,512,512]{2,1,0:T(8,128)(2,1)S(1)}, bf16[1,512,512]{2,1,0:T(8,128)(2,1)S(1)}, u32[]{:S(2)}, u32[]{:S(2)}) %collective-permute-start.2) | collective-permute-done | bytes 524320 | tf_op jit(solution)/shard_map/ppermute | solution.py:18
  136.3 0.8 multiply_convert_fusion.1
  137.6 1.1 copy-done.6
  138.7 1.3 fusion.17
  140.2 1.4 copy-done.11
  141.6 1.2 convert_bitcast_fusion.1
  142.9 1.5 collective-permute-start.3
  144.8 0.7 copy.76
  145.5 4.4 %copy.90 = bf16[2,8,128,1024]{3,1,2,0:T(8,128)(2,1)} copy(bf16[2,8,128,1024]{3,2,1,0:T(8,128)(2,1)S(1)} %bitcast.128) | data formatting | bytes 8388608
  149.9 0.6 copy.91
  150.5 1.6 collective-permute-done.3
  152.6 18.1 %pad_maximum_fusion = bf16[16,172032]{1,0:T(8,128)(2,1)} fusion(bf16[16,4096]{1,0:T(8,128)(2,1)S(1)} %convert_element_type.106, bf16[16,4096]{1,0:T(8,128)(2,1)S(1)} %convert_element_type.104, bf16[16,32768]{1,0:T(8,128)(2,1)S(1)} %bitcast.137, bf16[16,131072]{1,0:T(8,128)(2,1)} %bitcast.125), kind=kLoop, calls=%fused_computation | loop fusion | flops 22020096 | bytes 11010048 | tf_op jit(solution)/shard_map/concatenate | solution.py:80
  170.7 5.8 %reshape.206 = bf16[1024,2688]{1,0:T(8,128)(2,1)} reshape(bf16[16,172032]{1,0:T(8,128)(2,1)} %pad_maximum_fusion) | data formatting | bytes 11010048 | tf_op jit(solution)/shard_map/reshape | solution.py:82
  176.5 0.6 compare_select_fusion
  177.1 79.9 %reduce-scatter.2.cloned.1.call-done = bf16[64,2688]{1,0:T(8,128)(2,1)} async-done(((bf16[1024,2688]{1,0:T(8,128)(2,1)}), bf16[64,2688]{1,0:T(8,128)(2,1)}) %reduce-scatter.2.cloned.1.call-update) | async-done | bytes 344080 | tf_op jit(solution)/shard_map/reduce_scatter | solution.py:81
  257.1 1.4 reshape.207
  258.6 0.9 reshape.208
  259.4 0.7 reshape.209
  260.5 0.6 slice.897
  261.5 0.6 slice.898
  (295 shorter events, 10.9 us)
Async XLA Ops:
  7.2 6.9 %copy-start.10 = (f32[1,512,128]{2,1,0:T(8,128)S(1)}, f32[1,512,128]{2,1,0:T(8,128)}, u32[]{:S(2)}) copy-start(f32[1,512,128]{2,1,0:T(8,128)} %param.9) | copy-start | bytes 786436
  7.2 7.0 %copy-start.12 = (f32[1,512,128]{2,1,0:T(8,128)S(1)}, f32[1,512,128]{2,1,0:T(8,128)}, u32[]{:S(2)}) copy-start(f32[1,512,128]{2,1,0:T(8,128)} %param.8) | copy-start | bytes 786436
  7.2 64.2 %all-gather.4.cloned.1.call-start = ((), (), s32[]{:S(2)}) async-start(), calls=%async_computation.2 | async-start | bytes 5849088 | tf_op jit(solution)/shard_map/all_gather | solution.py:52
  11.3 245.7 %reduce-scatter.2.cloned.1.call-start = ((), (), s32[]{:S(2)}) async-start(), calls=%async_computation.1 | async-start | bytes 5849088 | tf_op jit(solution)/shard_map/reduce_scatter | solution.py:81
  83.0 9.4 %collective-permute-start = (bf16[1,256,512]{1,2,0:T(8,128)(2,1)S(1)}, bf16[1,256,512]{1,2,0:T(8,128)(2,1)S(1)}, u32[]{:S(2)}, u32[]{:S(2)}) collective-permute-start(bf16[1,256,512]{1,2,0:T(8,128)(2,1)S(1)} %get-tuple-element.17), channel_id=1, source_target_pairs={{0,2},{2,4},{4,6},{6,8},{8,10},{10,12},{12,14},{1,3},{3,5},{5,7},{... | collective-permute-start | bytes 786440 | tf_op jit(solution)/shard_map/ppermute | solution.py:18
  85.5 4.6 %slice-start = ((bf16[16,172032]{1,0:T(8,128)(2,1)}), bf16[16,32768]{1,0:T(8,128)(2,1)S(1)}, s32[]{:S(2)}) async-start(bf16[16,172032]{1,0:T(8,128)(2,1)} %reshape.213), calls=%async_computation.3 | async-start | bytes 2097152 | tf_op jit(solution)/shard_map/slice | solution.py:57
  92.2 2.2 copy-start.5
  92.3 21.9 %copy-start.9 = (bf16[1,16,32,512]{3,2,0,1:T(8,128)(2,1)}, bf16[1,16,32,512]{3,2,0,1:T(8,128)(2,1)S(1)}, u32[]{:S(2)}) copy-start(bf16[1,16,32,512]{3,2,0,1:T(8,128)(2,1)S(1)} %get-tuple-element.15) | copy-start | bytes 1572868
  92.3 0.8 copy-start.13
  94.4 1.4 copy-start.2
  95.8 15.6 %collective-permute-start.1 = (bf16[1,512,512]{1,2,0:T(8,128)(2,1)S(1)}, bf16[1,512,512]{1,2,0:T(8,128)(2,1)}, u32[]{:S(2)}, u32[]{:S(2)}) collective-permute-start(bf16[1,512,512]{1,2,0:T(8,128)(2,1)S(1)} %bitcast.132), channel_id=1, source_target_pairs={{0,2},{2,4},{4,6},{6,8},{8,10},{10,12},{12,14},{1,3},{3,5},{5,7},{... | collective-permute-start | bytes 1572872 | tf_op jit(solution)/shard_map/ppermute | solution.py:18
  101.7 9.7 %copy-start.7 = (bf16[1,16,64,1024]{3,2,0,1:T(8,128)(2,1)S(1)}, bf16[1,16,64,1024]{3,2,0,1:T(8,128)(2,1)}, u32[]{:S(2)}) copy-start(bf16[1,16,64,1024]{3,2,0,1:T(8,128)(2,1)} %get-tuple-element.10) | copy-start | bytes 6291460
  113.7 1.4 copy-start.4
  113.8 1.4 copy-start.14
  116.2 2.7 %copy-start.8 = (bf16[1,16,64,1024]{3,2,0,1:T(8,128)(2,1)S(1)}, bf16[1,16,64,1024]{3,2,0,1:T(8,128)(2,1)}, u32[]{:S(2)}) copy-start(bf16[1,16,64,1024]{3,2,0,1:T(8,128)(2,1)} %get-tuple-element.10) | copy-start | bytes 6291460
  120.3 15.7 %collective-permute-start.2 = (bf16[1,512,512]{2,1,0:T(8,128)(2,1)S(1)}, bf16[1,512,512]{2,1,0:T(8,128)(2,1)S(1)}, u32[]{:S(2)}, u32[]{:S(2)}) collective-permute-start(bf16[1,512,512]{2,1,0:T(8,128)(2,1)S(1)} %fusion.19), channel_id=1, source_target_pairs={{2,0},{4,2},{6,4},{8,6},{10,8},{12,10},{14,12},{3,1},{5,3},{7,5},{... | collective-permute-start | bytes 1572872 | tf_op jit(solution)/shard_map/ppermute | solution.py:18
  124.4 11.8 %copy-start.3 = (f32[512,1024]{1,0:T(8,128)S(1)}, f32[512,1024]{1,0:T(8,128)}, u32[]{:S(2)}) copy-start(f32[512,1024]{1,0:T(8,128)} %copy-done.2) | copy-start | bytes 6291460
  137.1 1.6 copy-start.6
  140.0 1.6 copy-start.11
  140.1 2.8 %copy-start = (f32[1,512,512]{2,1,0:T(8,128)}, f32[1,512,512]{2,1,0:T(8,128)S(1)}, u32[]{:S(2)}) copy-start(f32[1,512,512]{2,1,0:T(8,128)S(1)} %slice_bitcast_fusion) | copy-start | bytes 3145732
  142.9 9.3 %collective-permute-start.3 = (bf16[1,256,512]{2,1,0:T(8,128)(2,1)S(1)}, bf16[1,256,512]{2,1,0:T(8,128)(2,1)S(1)}, u32[]{:S(2)}, u32[]{:S(2)}) collective-permute-start(bf16[1,256,512]{2,1,0:T(8,128)(2,1)S(1)} %slice.1084), channel_id=1, source_target_pairs={{2,0},{4,2},{6,4},{8,6},{10,8},{12,10},{14,12},{3,1},{5,3},{7,5},{... | collective-permute-start | bytes 786440 | tf_op jit(solution)/shard_map/ppermute | solution.py:18
  149.8 2.3 slice-start.1
  257.1 3.1 %copy-start.1 = (bf16[64,2688]{1,0:T(8,128)(2,1)S(1)}, bf16[64,2688]{1,0:T(8,128)(2,1)}, u32[]{:S(2)}) copy-start(bf16[64,2688]{1,0:T(8,128)(2,1)} %reduce-scatter.2.cloned.1.call-done) | copy-start | bytes 1032196
Sparse Core Ops, SparseCore 0:
  11.4 59.9 all-gather.3
  176.6 80.3 reduce-scatter.1

commit v2 on v1

--- a/solution.py
+++ b/solution.py
@@ -56,7 +56,9 @@
         size = w.size
         piece = stacked[:, start : start + size]
         start += size
-        if w.ndim == 3:
+        if w.ndim == 4:
+            piece = piece.reshape((shard_devices,) + w.shape)
+        elif w.ndim == 3:
             piece = piece.reshape(shard_devices, w.shape[0], w.shape[1], w.shape[2])
             piece = piece.transpose(1, 0, 2, 3).reshape(
                 w.shape[0], shard_devices * w.shape[1], w.shape[2]
@@ -105,7 +107,21 @@
     within = lax.associative_scan(compose, (retain, inflow, forget), axis=1)
     summary = (within[0][:, -1], within[1][:, -1], within[2][:, -1])
     identity = (jnp.ones_like(summary[0]), jnp.zeros_like(summary[1]), jnp.zeros_like(summary[2]))
-    packed = lax.all_gather(jnp.stack(summary), "tm", axis=0, tiled=False)
+    summary_rest = jnp.stack(summary)
+    summary_parts = []
+    for _ in range(3):
+        part = summary_rest.astype(jnp.bfloat16)
+        summary_parts.append(part)
+        summary_rest = summary_rest - part.astype(jnp.float32)
+    summary_bits = jnp.stack(summary_parts, axis=-1)
+    conv_all, res_all, in_all, out_all, summary_all = gather_weights(
+        w_conv, w_res, w_in, w_out, summary_bits
+    )
+    summary_all = summary_all.astype(jnp.float32)
+    summary_all = (summary_all[..., 0] + summary_all[..., 1] + summary_all[..., 2]).reshape(
+        time_devices, site_devices, 3, site_count, band_count
+    )
+    packed = lax.dynamic_index_in_dim(summary_all, lax.axis_index("site"), 1, keepdims=False)
     shaped = tuple(packed[:, index] for index in range(3))
     inclusive = lax.associative_scan(compose, shaped, axis=0)
     position = lax.axis_index("tm")
@@ -123,7 +139,6 @@
     smoothed = mass_sum / weight_sum
     normed = (features / jnp.sqrt(smoothed + level_floor)).astype(jnp.bfloat16)
     flat_normed = normed.reshape(row_count, band_count)
-    conv_all, res_all, in_all, out_all = gather_weights(w_conv, w_res, w_in, w_out)
     channels = res_all.shape[1]
     hidden_now = jnp.dot(flat_normed, in_all, preferred_element_type=jnp.float32).astype(
         jnp.bfloat16

time: 270 us -> 318 us (1.18)
  waiting for transfers between devices: 125 us -> 196 us
  blocking collectives: 28.2 us -> 0 us
  local copies, waits for them, and re-layouts: 47.3 us -> 54.3 us
    all_gather x1, waiting for transfers between devices: 24.1 us -> 94 us  [gather_weights(): stacked = lax.all_gather(flat, ('tm', 'site'), axis=0, tiled=False)]
    all_gather x1 -> x0, blocking collectives: 28.2 us -> none  [on_device(): packed = lax.all_gather(jnp.stack(summary), 'tm', axis=0, tiled=False)]
    unnamed x37 -> x65, local copies, waits for them, and re-layouts: 16.7 us -> 28.5 us
    all_gather x1 -> x0, local copies, waits for them, and re-layouts: 5.64 us -> none  [gather_weights(): stacked = lax.all_gather(flat, ('tm', 'site'), axis=0, tiled=False)]
    slice x4 -> x3, local copies, waits for them, and re-layouts: 5.47 us -> 6.82 us  [gather_weights(): piece = stacked[:, start:start + size]]
  transfers between devices with their start and end apart: 6 -> 6, of which waited for: 5 -> 5; matrix products, arithmetic and copies ran while one was open for 9% -> 6% of each run, Pallas kernels for 0% -> 0%
where the time goes in v2:
time: 318 us; the launch traced here: 317 us
  waiting for transfers between devices  196 us (62%)
  local copies, waits for them, and re-layouts  54.3 us (17%)
  other arithmetic  26.4 us (8%)
  between operations  16.7 us (5%)
  matrix products  13.9 us (4%)
  starting transfers between devices  9.82 us (3%)
    all_gather x1, waiting for transfers between devices, gather_weights(): stacked = lax.all_gather(flat, ('tm', 'site'), axis=0, tiled=False)  94 us
    reduce_scatter x1, waiting for transfers between devices, scatter_terms(): lax.psum_scatter(joined_terms.reshape(shard_devices * 64, -1), ('tm', 'si...  80.3 us
    unnamed x65, local copies, waits for them, and re-layouts  28.5 us
    ppermute x4, waiting for transfers between devices, shifted(): return lax.ppermute(value, axis, pairs)  21.9 us
    concatenate x1, other arithmetic, scatter_terms(): joined_terms = jnp.concatenate(flat, axis=1)  18.4 us
    ppermute x4, starting transfers between devices, shifted(): return lax.ppermute(value, axis, pairs)  9.74 us
    slice x3, local copies, waits for them, and re-layouts, gather_weights(): piece = stacked[:, start:start + size]  6.82 us
  transfers between devices with their start and end apart: 6, of which 5 were waited for; matrix products, arithmetic and copies ran while one was open for 6% of the time, Pallas kernels for 0%

profile of v2, /device:TPU:0, one launch (start us, length us, event | category | flops | bytes accessed | tf_op | source)
XLA Modules:
  0.0 317.2 jit_solution(18103196571500419186)
XLA Ops:
  7.2 1.1 multiply_multiply_fusion
  13.9 4.7 %reshape.491 = bf16[1,1,173184]{2,1,0:T(2,128)(2,1)} reshape(bf16[173184]{0:T(1024)(128)(2,1)S(1)} %constant_dynamic-update-slice_fusion) | data formatting | bytes 692736
  18.7 94.0 %all-gather.4.cloned.1.call-done = bf16[16,1,173184]{2,1,0:T(2,128)(2,1)} async-done(((bf16[1,1,173184]{2,1,0:T(2,128)(2,1)}), bf16[16,1,173184]{2,1,0:T(2,128)(2,1)}) %all-gather.4.cloned.1.call-update) | async-done | bytes 5541904 | tf_op jit(solution)/shard_map/all_gather | solution.py:52
  112.7 6.1 %copy.52 = bf16[16,1,173184]{2,0,1:T(8,128)(2,1)S(1)} copy(bf16[16,1,173184]{2,1,0:T(2,128)(2,1)} %all-gather.4.cloned.1.call-done) | data formatting | bytes 11083776
  118.8 2.4 copy-done
  122.5 1.0 fusion.58
  123.5 4.5 %slice.898 = bf16[16,131072]{1,0:T(8,128)(2,1)} slice(bf16[16,173184]{1,0:T(8,128)(2,1)} %bitcast.134), slice={[0:16], [0:131072]} | slice | bytes 8388608 | tf_op jit(solution)/shard_map/slice | solution.py:57
  128.0 1.3 slice.902
  130.2 2.7 collective-permute-start
  132.8 4.5 %copy.47 = bf16[2,8,128,1024]{3,2,1,0:T(8,128)(2,1)S(1)} copy(bf16[2,8,128,1024]{3,1,2,0:T(8,128)(2,1)} %bitcast.136) | data formatting | bytes 8388608
  137.3 1.8 fusion.59
  139.6 0.9 copy-done.5
  140.5 1.3 fusion.15
  142.3 0.5 fusion
  143.2 4.3 %collective-permute-start.1 = (bf16[1,512,512]{1,2,0:T(8,128)(2,1)S(1)}, bf16[1,512,512]{1,2,0:T(8,128)(2,1)}, u32[]{:S(2)}, u32[]{:S(2)}) collective-permute-start(bf16[1,512,512]{1,2,0:T(8,128)(2,1)S(1)} %bitcast.143), channel_id=1, source_target_pairs={{0,2},{2,4},{4,6},{6,8},{8,10},{10,12},{12,14},{1,3},{3,5},{5,7},{... | collective-permute-start | bytes 1572872 | tf_op jit(solution)/shard_map/ppermute | solution.py:18
  148.2 1.1 pad_maximum_fusion.1
  149.3 8.6 %collective-permute-done.1 = bf16[1,512,512]{1,2,0:T(8,128)(2,1)} collective-permute-done((bf16[1,512,512]{1,2,0:T(8,128)(2,1)S(1)}, bf16[1,512,512]{1,2,0:T(8,128)(2,1)}, u32[]{:S(2)}, u32[]{:S(2)}) %collective-permute-start.1) | collective-permute-done | bytes 524320 | tf_op jit(solution)/shard_map/ppermute | solution.py:18
  157.9 2.3 fusion.13
  160.7 0.5 fusion.1
  162.2 0.9 multiply_convert_fusion.3
  163.1 1.3 fusion.18
  164.4 1.4 copy-done.11
  165.8 0.9 fusion.19
  166.7 1.5 collective-permute-start.2
  168.3 1.2 pad_maximum_fusion.2
  169.5 0.5 convolution_convert_fusion
  170.0 1.2 convert_bitcast_fusion
  171.2 11.4 %collective-permute-done.2 = bf16[1,512,512]{2,1,0:T(8,128)(2,1)} collective-permute-done((bf16[1,512,512]{2,1,0:T(8,128)(2,1)}, bf16[1,512,512]{2,1,0:T(8,128)(2,1)}, u32[]{:S(2)}, u32[]{:S(2)}) %collective-permute-start.2) | collective-permute-done | bytes 524320 | tf_op jit(solution)/shard_map/ppermute | solution.py:18
  182.7 1.3 fusion.4
  184.0 0.8 multiply_convert_fusion.1
  185.3 1.1 copy-done.6
  186.4 1.3 fusion.17
  187.9 1.4 copy-done.13
  189.3 1.2 convert_bitcast_fusion.1
  190.6 1.3 collective-permute-start.3
  192.3 0.7 copy.37
  193.0 4.4 %copy.49 = bf16[2,8,128,1024]{3,1,2,0:T(8,128)(2,1)} copy(bf16[2,8,128,1024]{3,2,1,0:T(8,128)(2,1)S(1)} %bitcast.139) | data formatting | bytes 8388608
  197.5 0.6 copy.50
  198.0 1.8 collective-permute-done.3
  200.3 18.4 %pad_maximum_fusion = bf16[16,172032]{1,0:T(8,128)(2,1)} fusion(bf16[16,4096]{1,0:T(8,128)(2,1)S(1)} %convert_element_type.207, bf16[16,4096]{1,0:T(8,128)(2,1)S(1)} %convert_element_type.205, bf16[16,32768]{1,0:T(8,128)(2,1)S(1)} %bitcast.149, bf16[16,131072]{1,0:T(8,128)(2,1)} %bitcast.137), kind=kLoop, calls=%fused_computation.1 | loop fusion | flops 22020096 | bytes 11010048 | tf_op jit(solution)/shard_map/concatenate | solution.py:82
  218.7 5.8 %reshape.483 = bf16[1024,2688]{1,0:T(8,128)(2,1)} reshape(bf16[16,172032]{1,0:T(8,128)(2,1)} %pad_maximum_fusion) | data formatting | bytes 11010048 | tf_op jit(solution)/shard_map/reshape | solution.py:84
  224.5 0.6 compare_select_fusion
  225.1 80.3 %reduce-scatter.2.cloned.1.call-done = bf16[64,2688]{1,0:T(8,128)(2,1)} async-done(((bf16[1024,2688]{1,0:T(8,128)(2,1)}), bf16[64,2688]{1,0:T(8,128)(2,1)}) %reduce-scatter.2.cloned.1.call-update) | async-done | bytes 344080 | tf_op jit(solution)/shard_map/reduce_scatter | solution.py:83
  305.3 1.4 reshape.484
  306.8 0.9 reshape.485
  307.7 0.7 reshape.486
  308.8 0.6 slice.917
  309.8 0.6 slice.918
  (330 shorter events, 11.6 us)
Async XLA Ops:
  7.2 1.5 copy-start.10
  7.2 105.5 %all-gather.4.cloned.1.call-start = ((), (), s32[]{:S(2)}) async-start(), calls=%async_computation.2 | async-start | bytes 11776512 | tf_op jit(solution)/shard_map/all_gather | solution.py:52
  12.7 1.0 copy-start.15
  12.8 1.0 copy-start.18
  12.8 1.0 copy-start.20
  12.9 1.0 copy-start.21
  18.6 286.7 %reduce-scatter.2.cloned.1.call-start = ((), (), s32[]{:S(2)}) async-start(), calls=%async_computation.1 | async-start | bytes 5849088 | tf_op jit(solution)/shard_map/reduce_scatter | solution.py:83
  118.8 2.4 copy-start
  128.0 1.7 copy-start.14
  130.2 9.4 %collective-permute-start = (bf16[1,256,512]{1,2,0:T(8,128)(2,1)S(1)}, bf16[1,256,512]{1,2,0:T(8,128)(2,1)S(1)}, u32[]{:S(2)}, u32[]{:S(2)}) collective-permute-start(bf16[1,256,512]{1,2,0:T(8,128)(2,1)S(1)} %get-tuple-element.19), channel_id=1, source_target_pairs={{0,2},{2,4},{4,6},{6,8},{8,10},{10,12},{12,14},{1,3},{3,5},{5,7},{... | collective-permute-start | bytes 786440 | tf_op jit(solution)/shard_map/ppermute | solution.py:18
  139.2 1.3 copy-start.5
  139.6 21.1 %copy-start.8 = (bf16[1,16,32,512]{3,2,0,1:T(8,128)(2,1)}, bf16[1,16,32,512]{3,2,0,1:T(8,128)(2,1)S(1)}, u32[]{:S(2)}) copy-start(bf16[1,16,32,512]{3,2,0,1:T(8,128)(2,1)S(1)} %get-tuple-element.17) | copy-start | bytes 1572868
  139.6 2.2 copy-start.16
  141.8 1.4 copy-start.3
  142.3 6.0 %copy-start.17 = (bf16[1,256,512]{1,2,0:T(8,128)(2,1)S(1)}, bf16[1,256,512]{1,2,0:T(8,128)(2,1)}, u32[]{:S(2)}) copy-start(bf16[1,256,512]{1,2,0:T(8,128)(2,1)} %copy-done.16) | copy-start | bytes 786436
  143.2 14.7 %collective-permute-start.1 = (bf16[1,512,512]{1,2,0:T(8,128)(2,1)S(1)}, bf16[1,512,512]{1,2,0:T(8,128)(2,1)}, u32[]{:S(2)}, u32[]{:S(2)}) collective-permute-start(bf16[1,512,512]{1,2,0:T(8,128)(2,1)S(1)} %bitcast.143), channel_id=1, source_target_pairs={{0,2},{2,4},{4,6},{6,8},{8,10},{10,12},{12,14},{1,3},{3,5},{5,7},{... | collective-permute-start | bytes 1572872 | tf_op jit(solution)/shard_map/ppermute | solution.py:18
  148.2 9.7 %copy-start.7 = (bf16[1,16,64,1024]{3,2,0,1:T(8,128)(2,1)S(1)}, bf16[1,16,64,1024]{3,2,0,1:T(8,128)(2,1)}, u32[]{:S(2)}) copy-start(bf16[1,16,64,1024]{3,2,0,1:T(8,128)(2,1)} %get-tuple-element.12) | copy-start | bytes 6291460
  160.2 1.0 copy-start.19
  161.2 1.0 copy-start.9
  163.1 1.3 copy-start.22
  163.1 1.3 copy-start.24
  164.4 1.4 copy-start.11
  166.7 16.0 %collective-permute-start.2 = (bf16[1,512,512]{2,1,0:T(8,128)(2,1)}, bf16[1,512,512]{2,1,0:T(8,128)(2,1)}, u32[]{:S(2)}, u32[]{:S(2)}) collective-permute-start(bf16[1,512,512]{2,1,0:T(8,128)(2,1)} %fusion.19), channel_id=1, source_target_pairs={{2,0},{4,2},{6,4},{8,6},{10,8},{12,10},{14,12},{3,1},{5,3},{7,5},{... | collective-permute-start | bytes 1572872 | tf_op jit(solution)/shard_map/ppermute | solution.py:18
  168.2 1.7 copy-start.23
  168.2 1.7 copy-start.25
  169.9 12.7 %copy-start.12 = (f32[512,1024]{1,0:T(8,128)S(1)}, f32[512,1024]{1,0:T(8,128)}, u32[]{:S(2)}) copy-start(f32[512,1024]{1,0:T(8,128)} %copy-done.11) | copy-start | bytes 6291460
  171.2 12.8 %copy-start.4 = (f32[512,1024]{1,0:T(8,128)S(1)}, f32[512,1024]{1,0:T(8,128)}, u32[]{:S(2)}) copy-start(f32[512,1024]{1,0:T(8,128)} %copy-done.3) | copy-start | bytes 6291460
  184.8 1.6 copy-start.6
  187.7 1.6 copy-start.13
  187.8 2.7 copy-start.1
  190.6 9.3 %collective-permute-start.3 = (bf16[1,256,512]{2,1,0:T(8,128)(2,1)S(1)}, bf16[1,256,512]{2,1,0:T(8,128)(2,1)S(1)}, u32[]{:S(2)}, u32[]{:S(2)}) collective-permute-start(bf16[1,256,512]{2,1,0:T(8,128)(2,1)S(1)} %slice.1107), channel_id=1, source_target_pairs={{2,0},{4,2},{6,4},{8,6},{10,8},{12,10},{14,12},{3,1},{5,3},{7,5},{... | collective-permute-start | bytes 786440 | tf_op jit(solution)/shard_map/ppermute | solution.py:18
  197.3 2.5 slice-start
  305.3 3.1 copy-start.2
Sparse Core Ops, SparseCore 0:
  18.8 93.9 all-gather.3
  224.6 80.6 reduce-scatter.1

commit v3 on v1

--- a/solution.py
+++ b/solution.py
@@ -77,9 +77,16 @@
         else:
             piece = t
         flat.append(piece.reshape(shard_devices, -1).astype(jnp.bfloat16))
+    time_devices = lax.axis_size("tm")
+    site_devices = lax.axis_size("site")
     joined_terms = jnp.concatenate(flat, axis=1)
+    width = joined_terms.shape[1]
+    by_site = joined_terms.reshape(time_devices, site_devices, width).transpose(1, 0, 2)
+    site_reduced = lax.psum_scatter(
+        by_site.reshape(site_devices * time_devices * 8, -1), "site", scatter_dimension=0, tiled=True
+    )
     reduced = lax.psum_scatter(
-        joined_terms.reshape(shard_devices * 64, -1), ("tm", "site"), scatter_dimension=0, tiled=True
+        site_reduced.reshape(time_devices * 64, -1), "tm", scatter_dimension=0, tiled=True
     ).astype(jnp.float32).reshape(-1)
     out = []
     start = 0

time: 270 us -> 299 us (1.11)
  local copies, waits for them, and re-layouts: 47.3 us -> 62.6 us
  other arithmetic: 26.1 us -> 32.1 us
  waiting for transfers between devices: 125 us -> 131 us
    transpose x0 -> x1, other arithmetic: none -> 23.2 us  [scatter_terms(): joined_terms.reshape(time_devices, site_devices, width).transpose(1, 0, 2)]
    concatenate x1 -> x0, other arithmetic: 18.1 us -> none  [scatter_terms(): joined_terms = jnp.concatenate(flat, axis=1)]
    convert_element_type x3 -> x5, local copies, waits for them, and re-layouts: 0.83 us -> 11.2 us  [scatter_terms(): flat.append(piece.reshape(shard_devices, -1).astype(jnp.bfloat16))]
    reduce_scatter x1 -> x2, waiting for transfers between devices: 79.9 us -> 88.2 us  [the longest x1 72.6 us: scatter_terms(): lax.psum_scatter(site_reduced.reshape(time_devices * 64, -1), 'tm', scatt...]
    unnamed x37, local copies, waits for them, and re-layouts: 16.7 us -> 9.91 us
    transpose x0 -> x1, local copies, waits for them, and re-layouts: none -> 5.56 us  [scatter_terms(): joined_terms.reshape(time_devices, site_devices, width).transpose(1, 0, 2)]
    reshape x2 -> x3, local copies, waits for them, and re-layouts: 7.23 us -> 11.9 us  [the longest x1 5.81 us: scatter_terms(): by_site.reshape(site_devices * time_devices * 8, -1)]
  transfers between devices with their start and end apart: 6 -> 7, of which waited for: 5 -> 5; matrix products, arithmetic and copies ran while one was open for 9% -> 11% of each run, Pallas kernels for 0% -> 0%
where the time goes in v3:
time: 299 us; the launch traced here: 298 us
  waiting for transfers between devices  131 us (44%)
  local copies, waits for them, and re-layouts  62.6 us (21%)
  other arithmetic  32.1 us (11%)
  blocking collectives  28.2 us (9%)
  matrix products  17.9 us (6%)
  between operations  16.1 us (5%)
  starting transfers between devices  10.6 us (4%)
    reduce_scatter x1, waiting for transfers between devices, scatter_terms(): lax.psum_scatter(site_reduced.reshape(time_devices * 64, -1), 'tm', scatt...  72.6 us
    all_gather x1, blocking collectives, on_device(): packed = lax.all_gather(jnp.stack(summary), 'tm', axis=0, tiled=False)  28.2 us
    all_gather x1, waiting for transfers between devices, gather_weights(): stacked = lax.all_gather(flat, ('tm', 'site'), axis=0, tiled=False)  24.1 us
    transpose x1, other arithmetic, scatter_terms(): joined_terms.reshape(time_devices, site_devices, width).transpose(1, 0, 2)  23.2 us
    ppermute x4, waiting for transfers between devices, shifted(): return lax.ppermute(value, axis, pairs)  18.3 us
    reduce_scatter x1, waiting for transfers between devices, scatter_terms(): lax.psum_scatter(by_site.reshape(site_devices * time_devices * 8, -1), 's...  15.5 us
    convert_element_type x5, local copies, waits for them, and re-layouts, scatter_terms(): flat.append(piece.reshape(shard_devices, -1).astype(jnp.bfloat16))  11.2 us
    ppermute x4, starting transfers between devices, shifted(): return lax.ppermute(value, axis, pairs)  10.4 us
  transfers between devices with their start and end apart: 7, of which 5 were waited for; matrix products, arithmetic and copies ran while one was open for 11% of the time, Pallas kernels for 0%

profile of v3, /device:TPU:0, one launch (start us, length us, event | category | flops | bytes accessed | tf_op | source)
XLA Modules:
  0.0 298.0 jit_solution(6056727643539154015)
XLA Ops:
  7.2 0.7 copy.104
  8.0 0.9 copy.103
  8.8 1.0 copy.102
  9.9 1.5 pad_maximum_fusion.8
  11.4 0.7 slice.693
  12.1 1.0 slice.694
  13.0 1.0 slice.734
  18.5 28.2 %all-gather = f32[24,1,128]{2,1,0:T(1,128)S(1)} all-gather(f32[3,1,128]{2,1,0:T(1,128)S(1)} %pad_maximum_fusion.32), channel_id=2, replica_groups=mesh['groups'=2,'tm'=8,'site'=2] {'tm'}, dimensions={0}, use_global_device_ids=true | all-gather | bytes 13824 | tf_op jit(solution)/shard_map/all_gather | solution.py:115
  47.3 24.1 %all-gather.4.cloned.1.call-done = bf16[2752512]{0:T(1024)(128)(2,1)} async-done(((bf16[172032]{0:T(1024)(128)(2,1)}), bf16[2752512]{0:T(1024)(128)(2,1)}) %all-gather.4.cloned.1.call-update) | async-done | bytes 5505040 | tf_op jit(solution)/shard_map/all_gather | solution.py:52
  71.4 5.6 %reshape.226 = bf16[16,172032]{1,0:T(8,128)(2,1)} reshape(bf16[2752512]{0:T(1024)(128)(2,1)} %all-gather.4.cloned.1.call-done) | data formatting | bytes 11010048 | tf_op jit(solution)/shard_map/all_gather | solution.py:52
  77.0 1.0 fusion.56
  78.0 4.5 %slice.878 = bf16[16,131072]{1,0:T(8,128)(2,1)} slice(bf16[16,172032]{1,0:T(8,128)(2,1)} %reshape.226), slice={[0:16], [0:131072]} | slice | bytes 8388608 | tf_op jit(solution)/shard_map/slice | solution.py:57
  83.0 2.5 collective-permute-start
  85.5 4.6 %copy.105 = bf16[2,8,128,1024]{3,2,1,0:T(8,128)(2,1)S(1)} copy(bf16[2,8,128,1024]{3,1,2,0:T(8,128)(2,1)} %bitcast.126) | data formatting | bytes 8388608
  90.4 1.8 fusion.57
  92.3 1.3 fusion.15
  95.0 5.1 %collective-permute-start.1 = (bf16[1,512,512]{1,2,0:T(8,128)(2,1)S(1)}, bf16[1,512,512]{1,2,0:T(8,128)(2,1)}, u32[]{:S(2)}, u32[]{:S(2)}) collective-permute-start(bf16[1,512,512]{1,2,0:T(8,128)(2,1)S(1)} %bitcast.131), channel_id=1, source_target_pairs={{0,2},{2,4},{4,6},{6,8},{8,10},{10,12},{12,14},{1,3},{3,5},{5,7},{... | collective-permute-start | bytes 1572872 | tf_op jit(solution)/shard_map/ppermute | solution.py:18
  100.9 2.1 pad_maximum_fusion
  103.0 7.6 %collective-permute-done.1 = bf16[1,512,512]{1,2,0:T(8,128)(2,1)} collective-permute-done((bf16[1,512,512]{1,2,0:T(8,128)(2,1)S(1)}, bf16[1,512,512]{1,2,0:T(8,128)(2,1)}, u32[]{:S(2)}, u32[]{:S(2)}) %collective-permute-start.1) | collective-permute-done | bytes 524320 | tf_op jit(solution)/shard_map/ppermute | solution.py:18
  110.6 2.3 fusion.13
  115.4 2.7 multiply_convert_fusion.3
  118.1 1.3 fusion.18
  119.5 1.3 collective-permute-start.2
  120.8 1.1 pad_maximum_fusion.1
  121.9 1.3 convolution_convert_fusion
  123.2 1.2 convert_bitcast_fusion
  124.4 10.7 %collective-permute-done.2 = bf16[1,512,512]{2,1,0:T(8,128)(2,1)S(1)} collective-permute-done((bf16[1,512,512]{2,1,0:T(8,128)(2,1)S(1)}, bf16[1,512,512]{2,1,0:T(8,128)(2,1)S(1)}, u32[]{:S(2)}, u32[]{:S(2)}) %collective-permute-start.2) | collective-permute-done | bytes 524320 | tf_op jit(solution)/shard_map/ppermute | solution.py:18
  135.5 0.8 multiply_convert_fusion.1
  136.8 1.1 copy-done.6
  137.9 1.3 fusion.17
  139.3 0.8 slice.1084
  140.0 0.8 slice.893
  141.2 1.2 convert_bitcast_fusion.1
  142.5 1.5 collective-permute-start.3
  144.4 2.5 copy.92
  146.8 7.9 %convert_element_type.102 = bf16[8,2,131072]{2,1,0:T(2,128)(2,1)} reshape(bf16[16,2,64,1024]{3,2,1,0:T(8,128)(2,1)} %copy.92) | data formatting | bytes 8388608 | tf_op jit(solution)/shard_map/convert_element_type | solution.py:79
  154.8 0.8 convert_element_type.104
  155.6 1.0 convert_element_type.105
  156.6 1.7 convolution_convert_fusion.4
  158.4 23.2 %maximum_bitcast_fusion = bf16[2,8,172032]{2,0,1:T(2,128)(2,1)S(1)} fusion(bf16[8,2,4096]{2,1,0:T(2,128)(2,1)S(1)} %convert_element_type.110, bf16[8,2,4096]{2,1,0:T(2,128)(2,1)S(1)} %convert_element_type.108, bf16[8,2,32768]{2,1,0:T(2,128)(2,1)S(1)} %convert_element_type.104, bf16[8,2,131072]{2,1,0:T(2,128)(2,1)} %convert_element_type.102), kind=kLoop, calls=%fused_computation | loop fusion | flops 22020096 | bytes 11010048 | tf_op jit(solution)/shard_map/transpose | solution.py:84
  181.6 5.6 %copy.95 = bf16[2,8,172032]{2,1,0:T(8,128)(2,1)} copy(bf16[2,8,172032]{2,0,1:T(2,128)(2,1)S(1)} %maximum_bitcast_fusion) | data formatting | bytes 11010048 | tf_op jit(solution)/shard_map/transpose | solution.py:84
  187.1 5.8 %reshape.218 = bf16[128,21504]{1,0:T(8,128)(2,1)} reshape(bf16[2,8,172032]{2,1,0:T(8,128)(2,1)} %copy.95) | data formatting | bytes 11010048 | tf_op jit(solution)/shard_map/reshape | solution.py:86
  193.0 15.5 %reduce-scatter.3.cloned.1.call-done = bf16[64,21504]{1,0:T(8,128)(2,1)} async-done(((bf16[128,21504]{1,0:T(8,128)(2,1)}), bf16[64,21504]{1,0:T(8,128)(2,1)}) %reduce-scatter.3.cloned.1.call-update) | async-done | bytes 2752528 | tf_op jit(solution)/shard_map/reduce_scatter | solution.py:85
  208.5 4.6 %reshape.219 = bf16[512,2688]{1,0:T(8,128)(2,1)} reshape(bf16[64,21504]{1,0:T(8,128)(2,1)} %reduce-scatter.3.cloned.1.call-done) | data formatting | bytes 5505024 | tf_op jit(solution)/shard_map/reshape | solution.py:89
  213.8 72.6 %reduce-scatter.5.cloned.1.call-done = bf16[64,2688]{1,0:T(8,128)(2,1)} async-done(((bf16[512,2688]{1,0:T(8,128)(2,1)}), bf16[64,2688]{1,0:T(8,128)(2,1)}) %reduce-scatter.5.cloned.1.call-update) | async-done | bytes 344080 | tf_op jit(solution)/shard_map/reduce_scatter | solution.py:88
  286.4 1.4 reshape.220
  287.9 0.9 reshape.221
  288.8 0.7 reshape.222
  (301 shorter events, 13.2 us)
Async XLA Ops:
  7.2 6.9 %copy-start.11 = (f32[1,512,128]{2,1,0:T(8,128)S(1)}, f32[1,512,128]{2,1,0:T(8,128)}, u32[]{:S(2)}) copy-start(f32[1,512,128]{2,1,0:T(8,128)} %param.9) | copy-start | bytes 786436
  7.2 7.0 %copy-start.13 = (f32[1,512,128]{2,1,0:T(8,128)S(1)}, f32[1,512,128]{2,1,0:T(8,128)}, u32[]{:S(2)}) copy-start(f32[1,512,128]{2,1,0:T(8,128)} %param.8) | copy-start | bytes 786436
  7.2 64.2 %all-gather.4.cloned.1.call-start = ((), (), s32[]{:S(2)}) async-start(), calls=%async_computation.4 | async-start | bytes 5849088 | tf_op jit(solution)/shard_map/all_gather | solution.py:52
  11.3 197.2 %reduce-scatter.3.cloned.1.call-start = ((), (), s32[]{:S(2)}) async-start(), calls=%async_computation.2 | async-start | bytes 8257536 | tf_op jit(solution)/shard_map/reduce_scatter | solution.py:85
  83.0 9.3 %collective-permute-start = (bf16[1,256,512]{1,2,0:T(8,128)(2,1)S(1)}, bf16[1,256,512]{1,2,0:T(8,128)(2,1)S(1)}, u32[]{:S(2)}, u32[]{:S(2)}) collective-permute-start(bf16[1,256,512]{1,2,0:T(8,128)(2,1)S(1)} %get-tuple-element.17), channel_id=1, source_target_pairs={{0,2},{2,4},{4,6},{6,8},{8,10},{10,12},{12,14},{1,3},{3,5},{5,7},{... | collective-permute-start | bytes 786440 | tf_op jit(solution)/shard_map/ppermute | solution.py:18
  85.5 4.6 %slice-start = ((bf16[16,172032]{1,0:T(8,128)(2,1)}), bf16[16,32768]{1,0:T(8,128)(2,1)S(1)}, s32[]{:S(2)}) async-start(bf16[16,172032]{1,0:T(8,128)(2,1)} %reshape.226), calls=%async_computation.5 | async-start | bytes 2097152 | tf_op jit(solution)/shard_map/slice | solution.py:57
  92.2 1.4 copy-start.5
  92.3 21.1 %copy-start.9 = (bf16[1,16,32,512]{3,2,0,1:T(8,128)(2,1)}, bf16[1,16,32,512]{3,2,0,1:T(8,128)(2,1)S(1)}, u32[]{:S(2)}) copy-start(bf16[1,16,32,512]{3,2,0,1:T(8,128)(2,1)S(1)} %get-tuple-element.15) | copy-start | bytes 1572868
  92.3 1.3 copy-start.14
  93.6 1.4 copy-start.1
  95.0 15.6 %collective-permute-start.1 = (bf16[1,512,512]{1,2,0:T(8,128)(2,1)S(1)}, bf16[1,512,512]{1,2,0:T(8,128)(2,1)}, u32[]{:S(2)}, u32[]{:S(2)}) collective-permute-start(bf16[1,512,512]{1,2,0:T(8,128)(2,1)S(1)} %bitcast.131), channel_id=1, source_target_pairs={{0,2},{2,4},{4,6},{6,8},{8,10},{10,12},{12,14},{1,3},{3,5},{5,7},{... | collective-permute-start | bytes 1572872 | tf_op jit(solution)/shard_map/ppermute | solution.py:18
  100.9 9.7 %copy-start.7 = (bf16[1,16,64,1024]{3,2,0,1:T(8,128)(2,1)S(1)}, bf16[1,16,64,1024]{3,2,0,1:T(8,128)(2,1)}, u32[]{:S(2)}) copy-start(bf16[1,16,64,1024]{3,2,0,1:T(8,128)(2,1)} %get-tuple-element.10) | copy-start | bytes 6291460
  112.9 1.4 copy-start.3
  113.0 1.4 copy-start.15
  115.4 2.7 copy-start.8
  119.5 15.7 %collective-permute-start.2 = (bf16[1,512,512]{2,1,0:T(8,128)(2,1)S(1)}, bf16[1,512,512]{2,1,0:T(8,128)(2,1)S(1)}, u32[]{:S(2)}, u32[]{:S(2)}) collective-permute-start(bf16[1,512,512]{2,1,0:T(8,128)(2,1)S(1)} %fusion.19), channel_id=1, source_target_pairs={{2,0},{4,2},{6,4},{8,6},{10,8},{12,10},{14,12},{3,1},{5,3},{7,5},{... | collective-permute-start | bytes 1572872 | tf_op jit(solution)/shard_map/ppermute | solution.py:18
  124.4 11.0 %copy-start.2 = (f32[512,1024]{1,0:T(8,128)S(1)}, f32[512,1024]{1,0:T(8,128)}, u32[]{:S(2)}) copy-start(f32[512,1024]{1,0:T(8,128)} %copy-done.1) | copy-start | bytes 6291460
  136.3 1.6 copy-start.6
  139.2 3.3 %copy-start.4 = (f32[512,1024]{1,0:T(8,128)}, f32[512,1024]{1,0:T(8,128)S(1)}, u32[]{:S(2)}) copy-start(f32[512,1024]{1,0:T(8,128)S(1)} %fusion.17) | copy-start | bytes 6291460
  139.2 2.0 copy-start.12
  142.5 13.2 %collective-permute-start.3 = (bf16[1,256,512]{2,1,0:T(8,128)(2,1)}, bf16[1,256,512]{2,1,0:T(8,128)(2,1)}, u32[]{:S(2)}, u32[]{:S(2)}) collective-permute-start(bf16[1,256,512]{2,1,0:T(8,128)(2,1)} %slice.1084), channel_id=1, source_target_pairs={{2,0},{4,2},{6,4},{8,6},{10,8},{12,10},{14,12},{3,1},{5,3},{7,5},{... | collective-permute-start | bytes 786440 | tf_op jit(solution)/shard_map/ppermute | solution.py:18
  146.8 7.9 %copy-start.10 = (bf16[512,512]{1,0:T(8,128)(2,1)S(1)}, bf16[512,512]{1,0:T(8,128)(2,1)}, u32[]{:S(2)}) copy-start(bf16[512,512]{1,0:T(8,128)(2,1)} %convolution_convert_fusion) | copy-start | bytes 1572868
  193.0 93.4 %reduce-scatter.5.cloned.1.call-start = ((), (), s32[]{:S(2)}) async-start(), calls=%async_computation.3 | async-start | bytes 3096576 | tf_op jit(solution)/shard_map/reduce_scatter | solution.py:88
  286.4 3.1 %copy-start = (bf16[64,2688]{1,0:T(8,128)(2,1)S(1)}, bf16[64,2688]{1,0:T(8,128)(2,1)}, u32[]{:S(2)}) copy-start(bf16[64,2688]{1,0:T(8,128)(2,1)} %reduce-scatter.5.cloned.1.call-done) | copy-start | bytes 1032196
Sparse Core Ops, SparseCore 0:
  11.4 59.9 all-gather.3
  193.1 15.4 reduce-scatter.2
  213.3 73.0 reduce-scatter.4
